TPU v7x, 256 devices: a whole 4x4x8 slice. The times are simulated.
256 devices in a mesh: dp: 8 (over z), context: 32 (over y, x, core).
Axes of the slice: x: 4, y: 4, z: 8, core: 2. Of those that a mesh axis runs over, the one named last changes fastest.
Arguments:
- query_in: bfloat16 [8, 16384, 1024], P('dp', 'context'), may hold values from -6 to 6
- key_in: bfloat16 [8, 16384, 1024], P('dp', 'context'), may hold values from -6 to 6
- value_in: bfloat16 [8, 16384, 1024], P('dp', 'context'), may hold values from -6 to 6
- out_grad: bfloat16 [8, 16384, 2048], P('dp', 'context'), may hold values from -6 to 6
- out_weight: bfloat16 [1024, 2048], P('context'), may hold values from -0.1875 to 0.1875
Outputs:
- output: bfloat16 [8, 16384, 2048], P('dp', 'context')
- query_grad: bfloat16 [8, 16384, 1024], P('dp', 'context')
- key_grad: bfloat16 [8, 16384, 1024], P('dp', 'context')
- value_grad: bfloat16 [8, 16384, 1024], P('dp', 'context')
- weight_grad: float32 [1024, 2048], P('context')
All inputs are finite; a program needn't handle non-finite values.
Results may differ from a plain program's by a relative error of at most 0.025.
Values may be sent and summed in bfloat16 or wider, within the bound.
No kernel may reach another device: no remote copies, remote signals or barrier semaphores. Data moves between devices by JAX's collectives and lax.ppermute only.
A program may use at most 192 MiB of HBM per device.

v0:
```python
import math
import jax
import jax.numpy as jnp
from jax import lax
from jax.sharding import PartitionSpec as P

HEADS = 8
HEAD_DIM = 128


def prefix(value, axis, join, neutral, backward):
    count, mine = (lax.axis_size(axis), lax.axis_index(axis))
    pieces = lax.all_gather(value, axis)
    if backward:
        pieces = pieces[::-1]
        mine = count - 1 - mine
    so_far = jnp.full_like(value, 0) + jnp.asarray(neutral, value.dtype)

    def turn(position, so_far):
        longer = join(so_far, pieces[position])
        return jnp.where(position < mine, longer, so_far)

    return lax.fori_loop(0, count - 1, turn, so_far)


def add_state(earlier, later):
    return earlier + later


def on_device(query_in, key_in, value_in, out_grad, out_weight):
    tok_rows = query_in.shape[1]
    head_width = query_in.shape[2]
    contexts = lax.axis_size("context")
    groups = lax.axis_size("dp")
    att_scale = 1.0 / math.sqrt(HEAD_DIM * tok_rows * contexts)
    grad_scale = 1.0 / math.sqrt(tok_rows * contexts * groups)
    split_heads = (tok_rows, HEADS, HEAD_DIM)
    queries = query_in[0].reshape(split_heads)
    keys_here = key_in[0].reshape(split_heads)
    values_here = value_in[0].reshape(split_heads)
    grad_flat = out_grad[0]
    full_weight = lax.all_gather(out_weight, "context", axis=0, tiled=True)
    head_grad = lax.dot_general(
        grad_flat, full_weight, (((1,), (1,)), ((), ())), preferred_element_type=jnp.float32
    ).astype(jnp.bfloat16)
    grad_heads = head_grad.reshape(split_heads)
    kv_block = jnp.einsum(
        "shd,she->hde", keys_here, values_here, preferred_element_type=jnp.float32
    )
    qg_block = jnp.einsum("thd,the->hde", queries, grad_heads, preferred_element_type=jnp.float32)
    blank_state = jnp.zeros_like(kv_block)
    kv_prior = prefix(kv_block, "context", add_state, blank_state, False)
    qg_later = prefix(qg_block, "context", add_state, blank_state, True)
    kv_before = kv_prior.astype(jnp.bfloat16)
    qg_after = qg_later.astype(jnp.bfloat16)
    positions = lax.broadcasted_iota(jnp.int32, (tok_rows, tok_rows), 0)
    sources = lax.broadcasted_iota(jnp.int32, (tok_rows, tok_rows), 1)
    causal = (positions >= sources)[None]
    scores = (
        jnp.einsum("thd,shd->hts", queries, keys_here, preferred_element_type=jnp.float32)
        * att_scale
    )
    scores = jnp.where(causal, scores, 0.0).astype(jnp.bfloat16)
    attended = jnp.einsum(
        "hts,shd->thd", scores, values_here, preferred_element_type=jnp.float32
    ) + att_scale * jnp.einsum(
        "thd,hde->the", queries, kv_before, preferred_element_type=jnp.float32
    )
    attended = attended.astype(jnp.bfloat16).reshape(tok_rows, head_width)
    output = jnp.dot(attended, full_weight, preferred_element_type=jnp.float32).astype(jnp.bfloat16)
    back_scores = (
        jnp.einsum("the,she->hts", grad_heads, values_here, preferred_element_type=jnp.float32)
        * att_scale
    )
    back_scores = jnp.where(causal, back_scores, 0.0).astype(jnp.bfloat16)
    query_grad = jnp.einsum(
        "hts,shd->thd", back_scores, keys_here, preferred_element_type=jnp.float32
    ) + att_scale * jnp.einsum(
        "the,hde->thd", grad_heads, kv_before, preferred_element_type=jnp.float32
    )
    key_grad = jnp.einsum(
        "hts,thd->shd", back_scores, queries, preferred_element_type=jnp.float32
    ) + att_scale * jnp.einsum(
        "she,hde->shd", values_here, qg_after, preferred_element_type=jnp.float32
    )
    value_grad = jnp.einsum(
        "hts,the->she", scores, grad_heads, preferred_element_type=jnp.float32
    ) + att_scale * jnp.einsum(
        "shd,hde->she", keys_here, qg_after, preferred_element_type=jnp.float32
    )
    query_grad = query_grad.astype(jnp.bfloat16).reshape(tok_rows, head_width)
    key_grad = key_grad.astype(jnp.bfloat16).reshape(tok_rows, head_width)
    value_grad = value_grad.astype(jnp.bfloat16).reshape(tok_rows, head_width)
    group_part = lax.psum_scatter(
        (
            lax.dot_general(
                attended, grad_flat, (((0,), (0,)), ((), ())), preferred_element_type=jnp.float32
            )
            * grad_scale
        ).astype(jnp.bfloat16),
        "context",
        scatter_dimension=0,
        tiled=True,
    )
    weight_grad = lax.psum(group_part, "dp").astype(jnp.float32)
    return (output[None], query_grad[None], key_grad[None], value_grad[None], weight_grad)


def solution(mesh):
    placed = (
        P("dp", "context", None),
        P("dp", "context", None),
        P("dp", "context", None),
        P("dp", "context", None),
        P("context", None),
    )
    return jax.shard_map(
        on_device,
        mesh=mesh,
        in_specs=placed,
        out_specs=(
            P("dp", "context", None),
            P("dp", "context", None),
            P("dp", "context", None),
            P("dp", "context", None),
            P("context", None),
        ),
        check_vma=False,
    )
```

profile of v0, /device:TPU:1, one launch (start us, length us, event | category | flops | bytes accessed | tf_op | source)
XLA Modules:
  0.0 466.4 jit_solution(10558739906381796081)
XLA Ops:
  7.2 1.6 copy.59
  8.9 2.9 copy.58
  11.7 2.4 copy.35
  14.1 2.5 fusion.16
  17.6 2.5 copy.57
  20.0 5.0 %select_convert_fusion.1 = bf16[8,512,512]{2,1,0:T(8,128)(2,1)} fusion(pred[512,512]{1,0:T(8,128)(4,1)S(1)} %iota_compare_fusion, bf16[512,8,128]{2,1,0:T(8,128)(2,1)} %bitcast.83, bf16[512,8,128]{2,1,0:T(8,128)(2,1)} %bitcast.78), kind=kOutput, calls=%fused_computation.4 | convolution fusion | flops 543162368 | bytes 6553600 | tf_op jit(solution)/shard_map/thd,shd->hts/dot_general | solution.py:60
  25.0 73.5 %all-gather.8.cloned.1.call-done = f32[256,128,128]{2,1,0:T(8,128)} async-done(((f32[8,128,128]{2,1,0:T(8,128)}), f32[256,128,128]{2,1,0:T(8,128)}) %all-gather.8.cloned.1.call-update) | async-done | bytes 16777232 | tf_op jit(solution)/shard_map/all_gather | solution.py:13
  98.5 38.9 %while.28 = (s32[]{:T(128)}, f32[8,128,128]{2,1,0:T(8,128)S(1)}, s32[]{:T(128)}, f32[32,8,128,128]{3,2,1,0:T(8,128)}, s32[]{:T(128)}, /*index=5*/s32[]{:T(128)}) while((s32[]{:T(128)}, f32[8,128,128]{2,1,0:T(8,128)S(1)}, s32[]{:T(128)}, f32[32,8,128,128]{3,2,1,0:T(8,128)}, s32[]{:T(128)}, /*index=5*/s32[]{:T(128)}) %tuple.81), condition=%wide.region_1.2_spmd.clone, body=%wide.region_0.1_spmd.clone.sunk | while | flops 393220 | bytes 1572957 | solution.py:23
  134.9 1.3 add_select_fusion.4
  137.5 1.8 fusion.21
  139.3 3.8 fusion.6
  144.2 4.3 multiply_convert_fusion
  148.6 3.2 all-gather.6.cloned.1.call-done
  151.7 5.5 %fusion.7 = bf16[512,1024]{1,0:T(8,128)(2,1)} fusion(bf16[1024,2048]{1,0:T(8,128)(2,1)} %all-gather.6.cloned.1.call-done, bf16[1,512,2048]{2,1,0:T(8,128)(2,1)S(1)} %copy-done), kind=kOutput, calls=%fused_computation.17 | convolution fusion | flops 2148007936 | bytes 7340032 | tf_op jit(solution)/shard_map/dot_general | solution.py:43
  157.3 1.6 copy.56
  158.9 83.8 %reduce-scatter.2.cloned.1.call-done = bf16[32,2048]{1,0:T(8,128)(2,1)} async-done(((bf16[1024,2048]{1,0:T(8,128)(2,1)}), bf16[32,2048]{1,0:T(8,128)(2,1)}) %reduce-scatter.2.cloned.1.call-update) | async-done | bytes 131088 | tf_op jit(solution)/shard_map/reduce_scatter | solution.py:94
  242.9 1.7 convolution_bitcast_fusion
  245.7 1.6 select_convert_fusion
  247.8 2.0 fusion.28
  250.5 1.5 fusion.2
  252.0 1.3 copy.51
  253.4 6.2 %fusion = bf16[1,512,2048]{2,1,0:T(8,128)(2,1)} fusion(bf16[512,1024]{0,1:T(8,128)(2,1)} %bitcast.92, bf16[1024,2048]{1,0:T(8,128)(2,1)} %all-gather.6.cloned.1.call-done), kind=kOutput, calls=%fused_computation.6 | convolution fusion | flops 2148532224 | bytes 7340032 | tf_op jit(solution)/shard_map/dot_general | solution.py:70
  259.6 53.3 %all-reduce.2.cloned.1.call-done = bf16[32,2048]{1,0:T(8,128)(2,1)} async-done(((bf16[32,2048]{1,0:T(8,128)(2,1)}), bf16[32,2048]{1,0:T(8,128)(2,1)}) %all-reduce.2.cloned.1.call-update) | async-done | bytes 131088 | tf_op jit(solution)/shard_map/psum | solution.py:105
  312.9 1.6 convert_element_type.51
  314.5 82.2 %all-gather.10.cloned.1.call-done = f32[256,128,128]{2,1,0:T(8,128)} async-done(((f32[8,128,128]{2,1,0:T(8,128)}), f32[256,128,128]{2,1,0:T(8,128)}) %all-gather.10.cloned.1.call-update) | async-done | bytes 16777232 | tf_op jit(solution)/shard_map/all_gather | solution.py:13
  396.7 11.6 %rev.3 = f32[32,8,128,128]{3,2,1,0:T(8,128)} reverse(f32[32,8,128,128]{3,2,1,0:T(8,128)} %bitcast.73), dimensions={0} | reverse | bytes 33554432 | tf_op jit(solution)/shard_map/rev | solution.py:15
  408.4 38.8 %while.29 = (s32[]{:T(128)}, f32[8,128,128]{2,1,0:T(8,128)S(1)}, s32[]{:T(128)}, f32[32,8,128,128]{3,2,1,0:T(8,128)}, s32[]{:T(128)}, /*index=5*/s32[]{:T(128)}) while((s32[]{:T(128)}, f32[8,128,128]{2,1,0:T(8,128)S(1)}, s32[]{:T(128)}, f32[32,8,128,128]{3,2,1,0:T(8,128)}, s32[]{:T(128)}, /*index=5*/s32[]{:T(128)}) %tuple.68), condition=%wide.region_3.4_spmd.clone, body=%wide.region_2.3_spmd.clone.sunk | while | flops 393220 | bytes 1572957 | solution.py:23
  408.4 1.3 add_select_fusion.5
  447.7 4.1 fusion.1
  451.8 2.4 copy.52
  454.2 3.5 add_convert_fusion
  457.6 2.3 copy.53
  (96 shorter events, 78.7 us)
Async XLA Ops:
  7.2 137.0 %copy-start = (bf16[1,512,2048]{2,1,0:T(8,128)(2,1)S(1)}, bf16[1,512,2048]{2,1,0:T(8,128)(2,1)}, u32[]{:S(2)}) copy-start(bf16[1,512,2048]{2,1,0:T(8,128)(2,1)} %param.12) | copy-start | bytes 6291460
  7.2 91.3 %all-gather.8.cloned.1.call-start = ((), (), s32[]{:S(2)}) async-start(), calls=%async_computation.4 | async-start | bytes 17301504 | tf_op jit(solution)/shard_map/all_gather | solution.py:13
  8.9 8.6 %copy-start.4 = (bf16[64,8,8,128]{3,2,1,0:T(8,128)(2,1)}, bf16[64,8,8,128]{3,2,1,0:T(8,128)(2,1)S(1)}, u32[]{:S(2)}) copy-start(bf16[64,8,8,128]{3,2,1,0:T(8,128)(2,1)S(1)} %copy.59) | copy-start | bytes 3145732
  16.6 135.1 %all-gather.6.cloned.1.call-start = ((), (), s32[]{:S(2)}) async-start(), calls=%async_computation.1 | async-start | bytes 4325376 | tf_op jit(solution)/shard_map/all_gather | solution.py:42
  17.4 225.3 %reduce-scatter.2.cloned.1.call-start = ((), (), s32[]{:S(2)}) async-start(), calls=%async_computation.2 | async-start | bytes 4325376 | tf_op jit(solution)/shard_map/reduce_scatter | solution.py:94
  137.5 1.8 copy-start.5
  143.1 1.1 copy-start.9
  148.5 164.4 %all-reduce.2.cloned.1.call-start = ((), (), s32[]{:S(2)}) async-start(), calls=%async_computation.3 | async-start | bytes 262144 | tf_op jit(solution)/shard_map/psum | solution.py:105
  157.3 88.4 %copy-start.6 = (bf16[64,8,8,128]{3,2,1,0:T(8,128)(2,1)S(1)}, bf16[64,8,8,128]{3,2,1,0:T(8,128)(2,1)}, u32[]{:S(2)}) copy-start(bf16[64,8,8,128]{3,2,1,0:T(8,128)(2,1)} %copy-done.4) | copy-start | bytes 3145732
  242.7 154.0 %all-gather.10.cloned.1.call-start = ((), (), s32[]{:S(2)}) async-start(), calls=%async_computation.5 | async-start | bytes 17301504 | tf_op jit(solution)/shard_map/all_gather | solution.py:13
  245.6 2.2 copy-start.2
  247.8 2.7 copy-start.3
  247.8 2.7 copy-start.8
  408.4 39.3 %copy-start.7 = (bf16[64,8,8,128]{3,2,1,0:T(8,128)(2,1)S(1)}, bf16[64,8,8,128]{3,2,1,0:T(8,128)(2,1)}, u32[]{:S(2)}) copy-start(bf16[64,8,8,128]{3,2,1,0:T(8,128)(2,1)} %copy.57) | copy-start | bytes 3145732
  451.8 8.1 %copy-start.1 = (bf16[1,512,2048]{2,1,0:T(8,128)(2,1)S(1)}, bf16[1,512,2048]{2,1,0:T(8,128)(2,1)}, u32[]{:S(2)}) copy-start(bf16[1,512,2048]{2,1,0:T(8,128)(2,1)} %param.12) | copy-start | bytes 6291460
Sparse Core Ops, SparseCore 0:
  16.8 81.7 all-gather.7
  101.1 50.6 all-gather.5
  155.7 86.9 reduce-scatter.1
  244.9 67.9 all-reduce.1
  315.3 81.3 all-gather.9
where the time goes:
time: 470 us; the launch traced here: 466 us
  waiting for transfers between devices  297 us (63%)
  other arithmetic  78 us (17%)
  matrix products  44.3 us (9%)
  local copies, waits for them, and re-layouts  31.5 us (7%)
  between operations  14 us (3%)
    all_gather x2, waiting for transfers between devices, prefix(): pieces = lax.all_gather(value, axis)  156 us
    reduce_scatter x1, waiting for transfers between devices, on_device(): lax.psum_scatter((lax.dot_general(attended, grad_flat, (((0,), (0,)), (()...  83.8 us
    select_n x62, other arithmetic, turn(): return jnp.where(position < mine, longer, so_far)  76.3 us
    psum x1, waiting for transfers between devices, on_device(): weight_grad = lax.psum(group_part, 'dp').astype(jnp.float32)  53.3 us
    unnamed x26, local copies, waits for them, and re-layouts  14.9 us
    rev x1, local copies, waits for them, and re-layouts, prefix(): pieces = pieces[::-1]  11.6 us
  transfers between devices with their start and end apart: 5, of which 5 were waited for; matrix products, arithmetic and copies ran while one was open for 17% of the time, Pallas kernels for 0%

commit v1 on v0

--- a/solution.py
+++ b/solution.py
@@ -102,7 +102,7 @@
         scatter_dimension=0,
         tiled=True,
     )
-    weight_grad = lax.psum(group_part, "dp").astype(jnp.float32)
+    weight_grad = jnp.sum(lax.all_gather(group_part, "dp"), axis=0).astype(jnp.float32)
     return (output[None], query_grad[None], key_grad[None], value_grad[None], weight_grad)
 
 

time: 470 us -> 400 us (0.85)
  waiting for transfers between devices: 297 us -> 226 us
    psum x1 -> x0, waiting for transfers between devices: 53.3 us -> none  [on_device(): weight_grad = lax.psum(group_part, 'dp').astype(jnp.float32)]
    reduce_scatter x1, waiting for transfers between devices: 83.8 us -> 66.8 us  [on_device(): lax.psum_scatter((lax.dot_general(attended, grad_flat, (((0,), (0,)), (()...]
  transfers between devices with their start and end apart: 5 -> 5, of which waited for: 5 -> 4; matrix products, arithmetic and copies ran while one was open for 17% -> 36% of each run, Pallas kernels for 0% -> 0%
where the time goes in v1:
time: 400 us; the launch traced here: 396 us
  waiting for transfers between devices  226 us (56%)
  other arithmetic  78.5 us (20%)
  matrix products  44.5 us (11%)
  local copies, waits for them, and re-layouts  31.5 us (8%)
  between operations  14 us (4%)
    all_gather x2, waiting for transfers between devices, prefix(): pieces = lax.all_gather(value, axis)  155 us
    select_n x62, other arithmetic, turn(): return jnp.where(position < mine, longer, so_far)  76.3 us
    reduce_scatter x1, waiting for transfers between devices, on_device(): lax.psum_scatter((lax.dot_general(attended, grad_flat, (((0,), (0,)), (()...  66.8 us
    unnamed x26, local copies, waits for them, and re-layouts  14.8 us
    rev x1, local copies, waits for them, and re-layouts, prefix(): pieces = pieces[::-1]  11.6 us
  transfers between devices with their start and end apart: 5, of which 4 were waited for; matrix products, arithmetic and copies ran while one was open for 36% of the time, Pallas kernels for 0%

profile of v1, /device:TPU:1, one launch (start us, length us, event | category | flops | bytes accessed | tf_op | source)
XLA Modules:
  0.0 396.2 jit_solution(10047399886816438667)
XLA Ops:
  7.2 1.6 copy.59
  8.9 2.9 copy.58
  11.7 2.4 copy.35
  14.1 2.5 fusion.16
  17.6 2.5 copy.57
  20.0 5.0 %select_convert_fusion.1 = bf16[8,512,512]{2,1,0:T(8,128)(2,1)} fusion(pred[512,512]{1,0:T(8,128)(4,1)S(1)} %iota_compare_fusion, bf16[512,8,128]{2,1,0:T(8,128)(2,1)} %bitcast.84, bf16[512,8,128]{2,1,0:T(8,128)(2,1)} %bitcast.79), kind=kOutput, calls=%fused_computation.4 | convolution fusion | flops 543162368 | bytes 6553600 | tf_op jit(solution)/shard_map/thd,shd->hts/dot_general | solution.py:60
  25.0 73.5 %all-gather.10.cloned.1.call-done = f32[256,128,128]{2,1,0:T(8,128)} async-done(((f32[8,128,128]{2,1,0:T(8,128)}), f32[256,128,128]{2,1,0:T(8,128)}) %all-gather.10.cloned.1.call-update) | async-done | bytes 16777232 | tf_op jit(solution)/shard_map/all_gather | solution.py:13
  98.5 38.9 %while.28 = (s32[]{:T(128)}, f32[8,128,128]{2,1,0:T(8,128)S(1)}, s32[]{:T(128)}, f32[32,8,128,128]{3,2,1,0:T(8,128)}, s32[]{:T(128)}, /*index=5*/s32[]{:T(128)}) while((s32[]{:T(128)}, f32[8,128,128]{2,1,0:T(8,128)S(1)}, s32[]{:T(128)}, f32[32,8,128,128]{3,2,1,0:T(8,128)}, s32[]{:T(128)}, /*index=5*/s32[]{:T(128)}) %tuple.81), condition=%wide.region_1.2_spmd.clone, body=%wide.region_0.1_spmd.clone.sunk | while | flops 393220 | bytes 1572957 | solution.py:23
  121.1 1.2 add_select_fusion.4
  134.9 1.3 add_select_fusion.4
  137.5 1.8 fusion.21
  139.3 3.8 fusion.6
  144.2 4.3 %multiply_convert_fusion = bf16[1024,2048]{1,0:T(8,128)(2,1)} fusion(bf16[512,1024]{0,1:T(8,128)(2,1)S(1)} %bitcast.93, bf16[1,512,2048]{2,1,0:T(8,128)(2,1)S(1)} %copy-done), kind=kOutput, calls=%fused_computation.2 | convolution fusion | flops 2151677952 | bytes 7340032 | tf_op jit(solution)/shard_map/dot_general | solution.py:96
  148.6 3.2 all-gather.8.cloned.1.call-done
  151.7 5.5 %fusion.7 = bf16[512,1024]{1,0:T(8,128)(2,1)} fusion(bf16[1024,2048]{1,0:T(8,128)(2,1)} %all-gather.8.cloned.1.call-done, bf16[1,512,2048]{2,1,0:T(8,128)(2,1)S(1)} %copy-done), kind=kOutput, calls=%fused_computation.17 | convolution fusion | flops 2148007936 | bytes 7340032 | tf_op jit(solution)/shard_map/dot_general | solution.py:43
  157.3 1.6 copy.56
  158.9 1.7 convolution_bitcast_fusion
  161.8 1.6 select_convert_fusion
  164.0 2.0 fusion.28
  166.7 1.5 fusion.2
  168.2 1.3 copy.51
  169.5 6.3 %fusion = bf16[1,512,2048]{2,1,0:T(8,128)(2,1)} fusion(bf16[512,1024]{0,1:T(8,128)(2,1)} %bitcast.94, bf16[1024,2048]{1,0:T(8,128)(2,1)} %all-gather.8.cloned.1.call-done), kind=kOutput, calls=%fused_computation.6 | convolution fusion | flops 2148532224 | bytes 7340032 | tf_op jit(solution)/shard_map/dot_general | solution.py:70
  175.9 66.8 %reduce-scatter.2.cloned.1.call-done = bf16[32,2048]{1,0:T(8,128)(2,1)} async-done(((bf16[1024,2048]{1,0:T(8,128)(2,1)}), bf16[32,2048]{1,0:T(8,128)(2,1)}) %reduce-scatter.2.cloned.1.call-update) | async-done | bytes 131088 | tf_op jit(solution)/shard_map/reduce_scatter | solution.py:94
  242.7 81.7 %all-gather.12.cloned.1.call-done = f32[256,128,128]{2,1,0:T(8,128)} async-done(((f32[8,128,128]{2,1,0:T(8,128)}), f32[256,128,128]{2,1,0:T(8,128)}) %all-gather.12.cloned.1.call-update) | async-done | bytes 16777232 | tf_op jit(solution)/shard_map/all_gather | solution.py:13
  324.4 11.6 %rev.3 = f32[32,8,128,128]{3,2,1,0:T(8,128)} reverse(f32[32,8,128,128]{3,2,1,0:T(8,128)} %bitcast.74), dimensions={0} | reverse | bytes 33554432 | tf_op jit(solution)/shard_map/rev | solution.py:15
  336.0 38.9 %while.29 = (s32[]{:T(128)}, f32[8,128,128]{2,1,0:T(8,128)S(1)}, s32[]{:T(128)}, f32[32,8,128,128]{3,2,1,0:T(8,128)}, s32[]{:T(128)}, /*index=5*/s32[]{:T(128)}) while((s32[]{:T(128)}, f32[8,128,128]{2,1,0:T(8,128)S(1)}, s32[]{:T(128)}, f32[32,8,128,128]{3,2,1,0:T(8,128)}, s32[]{:T(128)}, /*index=5*/s32[]{:T(128)}) %tuple.68), condition=%wide.region_3.4_spmd.clone, body=%wide.region_2.3_spmd.clone.sunk | while | flops 393220 | bytes 1572957 | solution.py:23
  336.0 1.3 add_select_fusion.5
  375.4 4.1 %fusion.1 = bf16[512,8,128]{0,2,1:T(8,128)(2,1)} fusion(f32[8,128,512]{2,1,0:T(8,128)S(1)} %fusion.13, bf16[8,512,512]{2,1,0:T(8,128)(2,1)} %copy-done.3, bf16[512,8,128]{2,1,0:T(8,128)(2,1)S(1)} %bitcast.82), kind=kOutput, calls=%fused_computation.8 | convolution fusion | flops 538443776 | bytes 8388608 | tf_op jit(solution)/shard_map/hts,thd->shd/dot_general | solution.py:81
  379.5 2.4 copy.52
  381.9 3.5 add_convert_fusion
  385.3 2.3 copy.53
  387.6 1.4 reduce_sum.12
  (97 shorter events, 78.1 us)
Async XLA Ops:
  7.2 137.0 %copy-start = (bf16[1,512,2048]{2,1,0:T(8,128)(2,1)S(1)}, bf16[1,512,2048]{2,1,0:T(8,128)(2,1)}, u32[]{:S(2)}) copy-start(bf16[1,512,2048]{2,1,0:T(8,128)(2,1)} %param.12) | copy-start | bytes 6291460
  7.2 91.3 %all-gather.10.cloned.1.call-start = ((), (), s32[]{:S(2)}) async-start(), calls=%async_computation.3 | async-start | bytes 17301504 | tf_op jit(solution)/shard_map/all_gather | solution.py:13
  8.9 8.6 %copy-start.4 = (bf16[64,8,8,128]{3,2,1,0:T(8,128)(2,1)}, bf16[64,8,8,128]{3,2,1,0:T(8,128)(2,1)S(1)}, u32[]{:S(2)}) copy-start(bf16[64,8,8,128]{3,2,1,0:T(8,128)(2,1)S(1)} %copy.59) | copy-start | bytes 3145732
  16.6 135.1 %all-gather.8.cloned.1.call-start = ((), (), s32[]{:S(2)}) async-start(), calls=%async_computation.1 | async-start | bytes 4325376 | tf_op jit(solution)/shard_map/all_gather | solution.py:42
  17.4 225.3 %reduce-scatter.2.cloned.1.call-start = ((), (), s32[]{:S(2)}) async-start(), calls=%async_computation.2 | async-start | bytes 4325376 | tf_op jit(solution)/shard_map/reduce_scatter | solution.py:94
  137.5 1.8 copy-start.5
  143.1 1.0 copy-start.9
  148.5 175.8 %all-gather.12.cloned.1.call-start = ((), (), s32[]{:S(2)}) async-start(), calls=%async_computation.4 | async-start | bytes 17301504 | tf_op jit(solution)/shard_map/all_gather | solution.py:13
  157.3 4.5 %copy-start.6 = (bf16[64,8,8,128]{3,2,1,0:T(8,128)(2,1)S(1)}, bf16[64,8,8,128]{3,2,1,0:T(8,128)(2,1)}, u32[]{:S(2)}) copy-start(bf16[64,8,8,128]{3,2,1,0:T(8,128)(2,1)} %copy-done.4) | copy-start | bytes 3145732
  161.6 226.0 %all-gather.14.cloned.1.call-start = ((), (), s32[]{:S(2)}) async-start(), calls=%async_computation.5 | async-start | bytes 1179648 | tf_op jit(solution)/shard_map/all_gather | solution.py:105
  161.8 2.2 copy-start.2
  164.0 2.7 copy-start.3
  164.0 2.7 copy-start.8
  336.0 39.4 %copy-start.7 = (bf16[64,8,8,128]{3,2,1,0:T(8,128)(2,1)S(1)}, bf16[64,8,8,128]{3,2,1,0:T(8,128)(2,1)}, u32[]{:S(2)}) copy-start(bf16[64,8,8,128]{3,2,1,0:T(8,128)(2,1)} %copy.57) | copy-start | bytes 3145732
  379.5 10.2 %copy-start.1 = (bf16[1,512,2048]{2,1,0:T(8,128)(2,1)S(1)}, bf16[1,512,2048]{2,1,0:T(8,128)(2,1)}, u32[]{:S(2)}) copy-start(bf16[1,512,2048]{2,1,0:T(8,128)(2,1)} %param.12) | copy-start | bytes 6291460
Sparse Core Ops, SparseCore 0:
  16.8 81.7 all-gather.9
  101.1 50.6 all-gather.7
  155.7 86.9 reduce-scatter.1
  245.4 78.9 all-gather.11
  326.1 32.7 all-gather.13
